TPU v7x, 32 devices: a whole 2x2x4 slice. The times are simulated.
32 devices in a mesh: row: 8 (over z, x), rep: 4 (over y, core).
Axes of the slice: x: 2, y: 2, z: 4, core: 2. Of those that a mesh axis runs over, the one named last changes fastest.
Arguments:
- features: bfloat16 [16384, 4096], P('row'), may hold values from -6 to 6
- coefficients: bfloat16 [4096, 512], P('row', 'rep'), may hold values from -0.1875 to 0.1875
- multiplicity: int32 [16384, 512], P('row', 'rep'), may hold values from 0 to 3
- treated: int32 [16384], P('row'), may hold values from 0 to 1
- outcome: int32 [16384], P('row'), may hold values from 0 to 1
- offset: float32 [16384], P('row'), may hold values from -4 to 4
- trim_low: int32 [512], P('rep'), may hold values from -768 to -256
- trim_high: int32 [512], P('rep'), may hold values from 256 to 768
Outputs:
- new_coefficients: float32 [4096, 512], P('row', 'rep')
- score: float32 [4096, 512], P('row', 'rep')
- effect: float32 [2, 4, 128], P(None, 'rep', 'row')
All inputs are finite; a program needn't handle non-finite values.
Results may differ from a plain program's by a relative error of at most 0.003.
Values may be sent and summed in bfloat16 or wider, within the bound.
A program may use at most 128 MiB of HBM per device.

v0:
```python
import jax
import jax.numpy as jnp
from jax import lax
from jax.sharding import PartitionSpec as P

REFIT_ITERS = 2


def newton_step(a_coef, c_coef, stats):
    ga = stats[0]
    gc = stats[1]
    s_all = stats[2]
    s_tr = stats[3]
    h11 = s_all + 1.0
    h22 = s_tr + 1.0
    det = h11 * h22 - s_tr * s_tr
    return (a_coef + (h22 * ga - s_tr * gc) / det, c_coef + (h11 * gc - s_tr * ga) / det)


def column_stats(a_coef, c_coef, ipw_t, treat, target, offset):
    prob = jax.nn.sigmoid(a_coef[:, None] + c_coef[:, None] * treat[None, :] + offset[None, :])
    res = ipw_t * (target[None, :] - prob)
    cur = ipw_t * prob * (1.0 - prob)
    return jnp.stack(
        [
            jnp.sum(res, axis=1),
            jnp.sum(res * treat[None, :], axis=1),
            jnp.sum(cur, axis=1),
            jnp.sum(cur * treat[None, :], axis=1),
        ]
    )


def local(features, coefficients, multiplicity, treated, outcome, offset, trim_low, trim_high):
    rep_block = coefficients.shape[1]
    cols = features
    logits = jnp.dot(
        cols,
        lax.all_gather(coefficients, "row", axis=0, tiled=True),
        preferred_element_type=jnp.float32,
    )
    low = trim_low.astype(jnp.float32) / 256.0
    high = trim_high.astype(jnp.float32) / 256.0
    prop = jax.nn.sigmoid(jnp.minimum(jnp.maximum(logits, low[None, :]), high[None, :]))
    weight = multiplicity.astype(jnp.float32)
    treat = treated.astype(jnp.float32)
    target = outcome.astype(jnp.float32)
    resid = (weight * (treat[:, None] - prop)).astype(jnp.bfloat16)
    curv = (weight * prop * (1.0 - prop)).astype(jnp.bfloat16)
    contract = (((0,), (0,)), ((), ()))
    cols = features
    grad = lax.psum_scatter(
        lax.dot_general(cols, resid, contract, preferred_element_type=jnp.float32),
        "row",
        scatter_dimension=0,
        tiled=True,
    )
    cols = features
    squared = (cols.astype(jnp.float32) * cols.astype(jnp.float32)).astype(jnp.bfloat16)
    hess = lax.psum_scatter(
        lax.dot_general(squared, curv, contract, preferred_element_type=jnp.float32),
        "row",
        scatter_dimension=0,
        tiled=True,
    )
    new_coefficients = coefficients.astype(jnp.float32) + grad / (hess + 1.0)
    score = grad / jnp.sqrt(hess + 1.0)
    prop_t = prop.T
    weight_t = weight.T
    ipw_t = weight_t * (treat[None, :] / prop_t + (1.0 - treat[None, :]) / (1.0 - prop_t))
    owned = rep_block // lax.axis_size("row")
    side = jnp.stack([treat, target, offset])
    side_all = lax.all_gather(side, "row", axis=1, tiled=True)
    mine = lax.all_to_all(ipw_t, "row", split_axis=0, concat_axis=1, tiled=True)
    a_coef = jnp.zeros((owned,), jnp.float32)
    c_coef = jnp.zeros((owned,), jnp.float32)
    for step in range(REFIT_ITERS):
        stats = column_stats(a_coef, c_coef, mine, side_all[0], side_all[1], side_all[2])
        a_coef, c_coef = newton_step(a_coef, c_coef, stats)
    result = jnp.stack([a_coef, c_coef])
    effect = result.reshape(2, 1, owned)
    return (new_coefficients, score, effect)


def solution(mesh):
    return jax.shard_map(
        local,
        mesh=mesh,
        in_specs=(
            P("row", None),
            P("row", "rep"),
            P("row", "rep"),
            P("row"),
            P("row"),
            P("row"),
            P("rep"),
            P("rep"),
        ),
        out_specs=(P("row", "rep"), P("row", "rep"), P(None, "rep", "row")),
        check_vma=False,
    )
```

profile of v0, /device:TPU:0, one launch (start us, length us, event | category | flops | bytes accessed | tf_op | source)
XLA Modules:
  0.0 235.5 jit_solution(13237240451449031860)
XLA Ops:
  7.2 0.0 all-gather.2.cloned.1.call-start
  7.2 0.7 all-gather.2.cloned.1.call-update
  7.9 0.0 reduce-scatter.3.cloned.1.call-start
  7.9 0.7 convert_element_type.33
  8.6 1.6 copy.12
  10.2 0.7 convert_multiply_fusion
  10.9 0.7 broadcast_subtract_fusion.1
  11.6 41.4 %all-gather.2.cloned.1.call-done = bf16[4096,128]{1,0:T(8,128)(2,1)} async-done(((bf16[512,128]{1,0:T(8,128)(2,1)}), bf16[4096,128]{1,0:T(8,128)(2,1)}) %all-gather.2.cloned.1.call-update) | async-done | bytes 1048592 | tf_op jit(solution)/shard_map/all_gather | solution.py:39
  53.0 12.9 %add_multiply_fusion = (f32[2048,128]{0,1:T(8,128)}, f32[2048,128]{0,1:T(8,128)S(1)}) fusion(s32[2048,128]{0,1:T(8,128)S(1)} %copy.12, f32[2048]{0:T(1024)S(1)} %broadcast_subtract_fusion.1, f32[2048]{0:T(1024)S(1)} %convert_element_type.33, f32[128]{0:T(128)S(1)} %get-tuple-element.31, f32[128]{0:T(128)S(1)} %get-tuple-element.32, ...), kind=kOutput, calls=%fused_computation.14 | convolution fusion | flops 2150367232 | bytes 20988928 | tf_op jit(solution)/shard_map/dot_general | solution.py:37
  65.9 9.5 %convolution_bitcast_fusion = f32[4096,128]{0,1:T(8,128)} fusion(bf16[2048,4096]{1,0:T(8,128)(2,1)} %param.8, s32[2048,128]{0,1:T(8,128)S(1)} %copy.12, f32[2048]{0:T(1024)S(1)} %convert_element_type.33, f32[2048,128]{0,1:T(8,128)S(1)} %get-tuple-element.30), kind=kOutput, calls=%fused_computation.2 | convolution fusion | flops 2148794368 | bytes 20979712 | tf_op jit(solution)/shard_map/dot_general | solution.py:53
  75.4 0.0 reduce-scatter.3.cloned.1.call-update
  75.4 0.0 copy-start
  75.5 0.0 copy-start.2
  75.5 0.0 copy-start.1
  75.5 0.0 reduce-scatter.5.cloned.1.call-start
  75.5 10.4 %fusion = f32[4096,128]{0,1:T(8,128)} fusion(bf16[2048,4096]{1,0:T(8,128)(2,1)} %param.8, s32[2048,128]{0,1:T(8,128)S(1)} %copy.12, f32[2048,128]{0,1:T(8,128)S(1)} %get-tuple-element.30), kind=kOutput, calls=%fused_computation.1 | convolution fusion | flops 2174222336 | bytes 20971520 | tf_op jit(solution)/shard_map/dot_general | solution.py:61
  86.0 0.0 reduce-scatter.5.cloned.1.call-update
  86.0 3.6 %all-to-all-start = ((f32[8,16,2048]{2,1,0:T(8,128)}), f32[8,16,2048]{2,1,0:T(8,128)S(1)}, u32[]{:S(2)}, u32[]{:S(2)}) async-start(f32[8,16,2048]{2,1,0:T(8,128)} %bitcast.2), calls=%async_computation.2 | async-start | bytes 2097152 | tf_op jit(solution)/shard_map/all_to_all | solution.py:74
  89.6 0.0 copy-done
  89.6 0.1 copy.11
  89.7 0.0 copy-done.2
  89.7 0.0 copy-done.1
  89.8 56.3 %all_gather.7 = f32[3,16384]{1,0:T(4,128)S(1)} all-gather(f32[3,2048]{1,0:T(4,128)S(1)} %pad_maximum_fusion), channel_id=1, replica_groups=mesh['row'=8,'rep'=4] {'row'}, dimensions={1}, use_global_device_ids=true | all-gather | bytes 221184 | tf_op jit(solution)/shard_map/all_gather | solution.py:73
  146.1 0.5 slice_reduce_fusion.2
  146.7 0.0 all-to-all-done
  146.7 0.7 fusion.8
  147.4 0.6 bitcast_multiply_fusion
  148.0 0.5 fusion.25
  148.5 0.6 pad_maximum_fusion.1
  149.1 6.5 %reduce-scatter.3.cloned.1.call-done = f32[512,128]{0,1:T(8,128)} async-done(((f32[4096,128]{0,1:T(8,128)}), f32[512,128]{0,1:T(8,128)}) %reduce-scatter.3.cloned.1.call-update) | async-done | bytes 262160 | tf_op jit(solution)/shard_map/reduce_scatter | solution.py:52
  155.6 70.6 %reduce-scatter.5.cloned.1.call-done = f32[512,128]{0,1:T(8,128)} async-done(((f32[4096,128]{0,1:T(8,128)}), f32[512,128]{0,1:T(8,128)}) %reduce-scatter.5.cloned.1.call-update) | async-done | bytes 262160 | tf_op jit(solution)/shard_map/reduce_scatter | solution.py:60
  226.2 1.1 rsqrt_multiply_fusion
  227.3 0.8 copy.14
  228.1 0.8 copy.15
  (9 shorter events, 0.2 us)
Async XLA Ops:
  7.2 45.9 %all-gather.2.cloned.1.call-start = ((), (), s32[]{:S(2)}) async-start(), calls=%async_computation.3 | async-start | bytes 1179648 | tf_op jit(solution)/shard_map/all_gather | solution.py:39
  7.9 147.7 %reduce-scatter.3.cloned.1.call-start = ((), (), s32[]{:S(2)}) async-start(), calls=%async_computation.4 | async-start | bytes 2359296 | tf_op jit(solution)/shard_map/reduce_scatter | solution.py:52
  75.4 14.1 %copy-start = (bf16[512,128]{1,0:T(8,128)(2,1)S(1)}, bf16[512,128]{1,0:T(8,128)(2,1)}, u32[]{:S(2)}) copy-start(bf16[512,128]{1,0:T(8,128)(2,1)} %param.9) | copy-start | bytes 393220
  75.5 14.2 %copy-start.2 = (s32[2048]{0:T(1024)S(1)}, s32[2048]{0:T(1024)}, u32[]{:S(2)}) copy-start(s32[2048]{0:T(1024)} %param.12) | copy-start | bytes 24580
  75.5 14.3 %copy-start.1 = (f32[2048]{0:T(1024)S(1)}, f32[2048]{0:T(1024)}, u32[]{:S(2)}) copy-start(f32[2048]{0:T(1024)} %param.13) | copy-start | bytes 24580
  75.5 150.7 %reduce-scatter.5.cloned.1.call-start = ((), (), s32[]{:S(2)}) async-start(), calls=%async_computation.5 | async-start | bytes 2359296 | tf_op jit(solution)/shard_map/reduce_scatter | solution.py:60
  86.0 60.7 %all-to-all-start = ((f32[8,16,2048]{2,1,0:T(8,128)}), f32[8,16,2048]{2,1,0:T(8,128)S(1)}, u32[]{:S(2)}, u32[]{:S(2)}) async-start(f32[8,16,2048]{2,1,0:T(8,128)} %bitcast.2), calls=%async_computation.2 | async-start | bytes 2097152 | tf_op jit(solution)/shard_map/all_to_all | solution.py:74
Sparse Core Ops, SparseCore 0:
  10.1 42.8 all-gather.1
  75.6 79.9 reduce-scatter.2
  159.1 67.0 reduce-scatter.4
where the time goes:
time: 236 us; the launch traced here: 235 us
  waiting for transfers between devices  119 us (50%)
  blocking collectives  56.3 us (24%)
  matrix products  32.8 us (14%)
  between operations  13.9 us (6%)
  other arithmetic  5.6 us (2%)
  local copies, waits for them, and re-layouts  3.92 us (2%)
  starting transfers between devices  3.69 us (2%)
    reduce_scatter x1, waiting for transfers between devices, local(): lax.psum_scatter(lax.dot_general(squared, curv, contract, preferred_eleme...  70.6 us
    all_gather x1, blocking collectives, local(): side_all = lax.all_gather(side, 'row', axis=1, tiled=True)  56.3 us
    all_gather x1, waiting for transfers between devices, local(): lax.all_gather(coefficients, 'row', axis=0, tiled=True)  41.4 us
    dot_general x1, matrix products, local(): jnp.dot(cols, lax.all_gather(coefficients, 'row', axis=0, tiled=True), pr...  12.9 us
    dot_general x1, matrix products, local(): lax.dot_general(squared, curv, contract, preferred_element_type=jnp.float32)  10.4 us
    dot_general x1, matrix products, local(): lax.dot_general(cols, resid, contract, preferred_element_type=jnp.float32)  9.49 us
    reduce_scatter x1, waiting for transfers between devices, local(): lax.psum_scatter(lax.dot_general(cols, resid, contract, preferred_element...  6.49 us
  transfers between devices with their start and end apart: 4, of which 3 were waited for; matrix products, arithmetic and copies ran while one was open for 7% of the time, Pallas kernels for 0%

commit v1 on v0

--- a/solution.py
+++ b/solution.py
@@ -70,7 +70,12 @@
     ipw_t = weight_t * (treat[None, :] / prop_t + (1.0 - treat[None, :]) / (1.0 - prop_t))
     owned = rep_block // lax.axis_size("row")
     side = jnp.stack([treat, target, offset])
-    side_all = lax.all_gather(side, "row", axis=1, tiled=True)
+    ring = [side]
+    for hop in range(7):
+        ring.append(lax.ppermute(ring[-1], "row", [(dev, (dev + 1) % 8) for dev in range(8)]))
+    side_all = jnp.roll(
+        jnp.concatenate(ring[::-1], axis=1), (lax.axis_index("row") + 1) * ring[0].shape[1], axis=1
+    )
     mine = lax.all_to_all(ipw_t, "row", split_axis=0, concat_axis=1, tiled=True)
     a_coef = jnp.zeros((owned,), jnp.float32)
     c_coef = jnp.zeros((owned,), jnp.float32)

time: 236 us -> 233 us (0.987)
  blocking collectives: 56.3 us -> 0 us
  waiting for transfers between devices: 119 us -> 171 us
    all_gather x1 -> x0, blocking collectives: 56.3 us -> none  [local(): side_all = lax.all_gather(side, 'row', axis=1, tiled=True)]
    ppermute x0 -> x7, waiting for transfers between devices: none -> 48.2 us  [local(): lax.ppermute(ring[-1], 'row', [(dev, (dev + 1) % 8) for dev in range(8)])]
    all_to_all x1, waiting for transfers between devices: 0.01 us -> 23.6 us  [local(): mine = lax.all_to_all(ipw_t, 'row', split_axis=0, concat_axis=1, tiled=True)]
    reduce_scatter x1, waiting for transfers between devices: 70.6 us -> 56.7 us  [local(): lax.psum_scatter(lax.dot_general(squared, curv, contract, preferred_eleme...]
    reduce_scatter x1, waiting for transfers between devices: 6.49 us -> 0.01 us  [local(): lax.psum_scatter(lax.dot_general(cols, resid, contract, preferred_element...]
  transfers between devices with their start and end apart: 4 -> 11, of which waited for: 3 -> 10; matrix products, arithmetic and copies ran while one was open for 7% -> 8% of each run, Pallas kernels for 0% -> 0%
where the time goes in v1:
time: 233 us; the launch traced here: 232 us
  waiting for transfers between devices  171 us (73%)
  matrix products  33.2 us (14%)
  between operations  13.9 us (6%)
  other arithmetic  5.76 us (2%)
  starting transfers between devices  4.49 us (2%)
  local copies, waits for them, and re-layouts  4.18 us (2%)
    reduce_scatter x1, waiting for transfers between devices, local(): lax.psum_scatter(lax.dot_general(squared, curv, contract, preferred_eleme...  56.7 us
    ppermute x7, waiting for transfers between devices, local(): lax.ppermute(ring[-1], 'row', [(dev, (dev + 1) % 8) for dev in range(8)])  48.2 us
    all_gather x1, waiting for transfers between devices, local(): lax.all_gather(coefficients, 'row', axis=0, tiled=True)  41.4 us
    all_to_all x1, waiting for transfers between devices, local(): mine = lax.all_to_all(ipw_t, 'row', split_axis=0, concat_axis=1, tiled=True)  23.6 us
    dot_general x1, matrix products, local(): jnp.dot(cols, lax.all_gather(coefficients, 'row', axis=0, tiled=True), pr...  12.9 us
    dot_general x1, matrix products, local(): lax.dot_general(squared, curv, contract, preferred_element_type=jnp.float32)  10.7 us
    dot_general x1, matrix products, local(): lax.dot_general(cols, resid, contract, preferred_element_type=jnp.float32)  9.65 us
  transfers between devices with their start and end apart: 11, of which 10 were waited for; matrix products, arithmetic and copies ran while one was open for 8% of the time, Pallas kernels for 0%

profile of v1, /device:TPU:0, one launch (start us, length us, event | category | flops | bytes accessed | tf_op | source)
XLA Modules:
  0.0 232.2 jit_solution(2338691269057218759)
XLA Ops:
  7.2 0.0 all-gather.2.cloned.1.call-start
  7.2 0.7 all-gather.2.cloned.1.call-update
  7.9 0.0 reduce-scatter.3.cloned.1.call-start
  7.9 0.7 convert_element_type.33
  8.6 1.6 copy.12
  10.2 0.7 convert_multiply_fusion
  10.9 0.7 broadcast_subtract_fusion.1
  11.6 41.4 %all-gather.2.cloned.1.call-done = bf16[4096,128]{1,0:T(8,128)(2,1)} async-done(((bf16[512,128]{1,0:T(8,128)(2,1)}), bf16[4096,128]{1,0:T(8,128)(2,1)}) %all-gather.2.cloned.1.call-update) | async-done | bytes 1048592 | tf_op jit(solution)/shard_map/all_gather | solution.py:39
  53.0 12.9 %add_multiply_fusion = (f32[2048,128]{0,1:T(8,128)}, f32[2048,128]{0,1:T(8,128)S(1)}) fusion(s32[2048,128]{0,1:T(8,128)S(1)} %copy.12, f32[2048]{0:T(1024)S(1)} %broadcast_subtract_fusion.1, f32[2048]{0:T(1024)S(1)} %convert_element_type.33, f32[128]{0:T(128)S(1)} %get-tuple-element.31, f32[128]{0:T(128)S(1)} %get-tuple-element.32, ...), kind=kOutput, calls=%fused_computation.14 | convolution fusion | flops 2150367232 | bytes 20988928 | tf_op jit(solution)/shard_map/dot_general | solution.py:37
  65.9 0.0 copy-start.2
  66.0 0.0 copy-start.1
  66.0 0.0 copy-start
  66.0 9.6 %convolution_bitcast_fusion = f32[4096,128]{0,1:T(8,128)} fusion(bf16[2048,4096]{1,0:T(8,128)(2,1)} %param.8, s32[2048,128]{0,1:T(8,128)S(1)} %copy.12, f32[2048]{0:T(1024)S(1)} %convert_element_type.33, f32[2048,128]{0,1:T(8,128)S(1)} %get-tuple-element.30), kind=kOutput, calls=%fused_computation.2 | convolution fusion | flops 2148794368 | bytes 20979712 | tf_op jit(solution)/shard_map/dot_general | solution.py:53
  75.6 0.0 reduce-scatter.3.cloned.1.call-update
  75.6 0.0 reduce-scatter.5.cloned.1.call-start
  75.7 0.0 copy-done.2
  75.7 0.0 copy-done.1
  75.7 0.6 collective-permute-start
  76.3 6.1 %collective-permute-done = f32[3,2048]{1,0:T(4,128)S(1)} collective-permute-done((f32[3,2048]{1,0:T(4,128)S(1)}, f32[3,2048]{1,0:T(4,128)S(1)}, u32[]{:S(2)}, u32[]{:S(2)}) %collective-permute-start) | collective-permute-done | bytes 24608 | tf_op jit(solution)/shard_map/ppermute | solution.py:75
  82.4 0.0 collective-permute-start.1
  82.4 7.2 %collective-permute-done.1 = f32[3,2048]{1,0:T(4,128)S(1)} collective-permute-done((f32[3,2048]{1,0:T(4,128)S(1)}, f32[3,2048]{1,0:T(4,128)S(1)}, u32[]{:S(2)}, u32[]{:S(2)}) %collective-permute-start.1) | collective-permute-done | bytes 24608 | tf_op jit(solution)/shard_map/ppermute | solution.py:75
  89.6 0.0 collective-permute-start.2
  89.6 7.4 %collective-permute-done.2 = f32[3,2048]{1,0:T(4,128)S(1)} collective-permute-done((f32[3,2048]{1,0:T(4,128)S(1)}, f32[3,2048]{1,0:T(4,128)S(1)}, u32[]{:S(2)}, u32[]{:S(2)}) %collective-permute-start.2) | collective-permute-done | bytes 24608 | tf_op jit(solution)/shard_map/ppermute | solution.py:75
  97.0 0.0 collective-permute-start.3
  97.0 7.7 %collective-permute-done.3 = f32[3,2048]{1,0:T(4,128)S(1)} collective-permute-done((f32[3,2048]{1,0:T(4,128)S(1)}, f32[3,2048]{1,0:T(4,128)S(1)}, u32[]{:S(2)}, u32[]{:S(2)}) %collective-permute-start.3) | collective-permute-done | bytes 24608 | tf_op jit(solution)/shard_map/ppermute | solution.py:75
  104.7 0.0 collective-permute-start.4
  104.7 6.7 %collective-permute-done.4 = f32[3,2048]{1,0:T(4,128)S(1)} collective-permute-done((f32[3,2048]{1,0:T(4,128)S(1)}, f32[3,2048]{1,0:T(4,128)S(1)}, u32[]{:S(2)}, u32[]{:S(2)}) %collective-permute-start.4) | collective-permute-done | bytes 24608 | tf_op jit(solution)/shard_map/ppermute | solution.py:75
  111.4 0.0 collective-permute-start.5
  111.4 6.7 %collective-permute-done.5 = f32[3,2048]{1,0:T(4,128)S(1)} collective-permute-done((f32[3,2048]{1,0:T(4,128)S(1)}, f32[3,2048]{1,0:T(4,128)S(1)}, u32[]{:S(2)}, u32[]{:S(2)}) %collective-permute-start.5) | collective-permute-done | bytes 24608 | tf_op jit(solution)/shard_map/ppermute | solution.py:75
  118.1 0.0 collective-permute-start.6
  118.1 0.0 copy-done
  118.1 0.1 copy.11
  118.2 6.5 %collective-permute-done.6 = f32[3,2048]{1,0:T(4,128)S(1)} collective-permute-done((f32[3,2048]{1,0:T(4,128)S(1)}, f32[3,2048]{1,0:T(4,128)S(1)}, u32[]{:S(2)}, u32[]{:S(2)}) %collective-permute-start.6) | collective-permute-done | bytes 24608 | tf_op jit(solution)/shard_map/ppermute | solution.py:75
  124.9 10.7 %fusion = f32[4096,128]{0,1:T(8,128)} fusion(bf16[2048,4096]{1,0:T(8,128)(2,1)} %param.8, s32[2048,128]{0,1:T(8,128)S(1)} %copy.12, f32[2048,128]{0,1:T(8,128)S(1)} %get-tuple-element.30), kind=kOutput, calls=%fused_computation.1 | convolution fusion | flops 2174222336 | bytes 20971520 | tf_op jit(solution)/shard_map/dot_general | solution.py:61
  135.5 0.0 reduce-scatter.5.cloned.1.call-update
  135.6 3.8 %all-to-all-start = ((f32[8,16,2048]{2,1,0:T(8,128)}), f32[8,16,2048]{2,1,0:T(8,128)S(1)}, u32[]{:S(2)}, u32[]{:S(2)}) async-start(f32[8,16,2048]{2,1,0:T(8,128)} %bitcast.2), calls=%async_computation.2 | async-start | bytes 2097152 | tf_op jit(solution)/shard_map/all_to_all | solution.py:79
  139.5 0.6 dynamic-slice_reduce_fusion.2
  140.2 23.6 %all-to-all-done = f32[8,16,2048]{2,1,0:T(8,128)S(1)} async-done(((f32[8,16,2048]{2,1,0:T(8,128)}), f32[8,16,2048]{2,1,0:T(8,128)S(1)}, u32[]{:S(2)}, u32[]{:S(2)}) %all-to-all-start) | async-done | bytes 1048608 | tf_op jit(solution)/shard_map/all_to_all | solution.py:79
  163.8 0.7 fusion.8
  164.5 0.6 bitcast_multiply_fusion
  165.1 0.5 fusion.25
  165.6 0.6 pad_maximum_fusion.1
  166.2 0.0 reduce-scatter.3.cloned.1.call-done
  166.2 56.7 %reduce-scatter.5.cloned.1.call-done = f32[512,128]{0,1:T(8,128)} async-done(((f32[4096,128]{0,1:T(8,128)}), f32[512,128]{0,1:T(8,128)}) %reduce-scatter.5.cloned.1.call-update) | async-done | bytes 262160 | tf_op jit(solution)/shard_map/reduce_scatter | solution.py:60
  222.9 1.1 rsqrt_multiply_fusion
  224.0 0.8 copy.14
  224.9 0.8 copy.15
  (25 shorter events, 0.4 us)
Async XLA Ops:
  7.2 45.9 %all-gather.2.cloned.1.call-start = ((), (), s32[]{:S(2)}) async-start(), calls=%async_computation.3 | async-start | bytes 1179648 | tf_op jit(solution)/shard_map/all_gather | solution.py:39
  7.9 158.3 %reduce-scatter.3.cloned.1.call-start = ((), (), s32[]{:S(2)}) async-start(), calls=%async_computation.4 | async-start | bytes 2359296 | tf_op jit(solution)/shard_map/reduce_scatter | solution.py:52
  65.9 9.7 %copy-start.2 = (s32[2048]{0:T(1024)S(1)}, s32[2048]{0:T(1024)}, u32[]{:S(2)}) copy-start(s32[2048]{0:T(1024)} %param.12) | copy-start | bytes 24580
  66.0 9.7 %copy-start.1 = (f32[2048]{0:T(1024)S(1)}, f32[2048]{0:T(1024)}, u32[]{:S(2)}) copy-start(f32[2048]{0:T(1024)} %param.13) | copy-start | bytes 24580
  66.0 52.2 %copy-start = (bf16[512,128]{1,0:T(8,128)(2,1)S(1)}, bf16[512,128]{1,0:T(8,128)(2,1)}, u32[]{:S(2)}) copy-start(bf16[512,128]{1,0:T(8,128)(2,1)} %param.9) | copy-start | bytes 393220
  75.6 147.3 %reduce-scatter.5.cloned.1.call-start = ((), (), s32[]{:S(2)}) async-start(), calls=%async_computation.5 | async-start | bytes 2359296 | tf_op jit(solution)/shard_map/reduce_scatter | solution.py:60
  75.7 6.7 %collective-permute-start = (f32[3,2048]{1,0:T(4,128)S(1)}, f32[3,2048]{1,0:T(4,128)S(1)}, u32[]{:S(2)}, u32[]{:S(2)}) collective-permute-start(f32[3,2048]{1,0:T(4,128)S(1)} %pad_maximum_fusion), channel_id=1, source_target_pairs={{0,4},{4,8},{8,12},{12,16},{16,20},{20,24},{24,28},{28,0},{1,5},{5... | collective-permute-start | bytes 73736 | tf_op jit(solution)/shard_map/ppermute | solution.py:75
  82.4 7.2 %collective-permute-start.1 = (f32[3,2048]{1,0:T(4,128)S(1)}, f32[3,2048]{1,0:T(4,128)S(1)}, u32[]{:S(2)}, u32[]{:S(2)}) collective-permute-start(f32[3,2048]{1,0:T(4,128)S(1)} %collective-permute-done), channel_id=1, source_target_pairs={{0,4},{4,8},{8,12},{12,16},{16,20},{20,24},{24,28},{28,0},{1,5},{5... | collective-permute-start | bytes 73736 | tf_op jit(solution)/shard_map/ppermute | solution.py:75
  89.6 7.4 %collective-permute-start.2 = (f32[3,2048]{1,0:T(4,128)S(1)}, f32[3,2048]{1,0:T(4,128)S(1)}, u32[]{:S(2)}, u32[]{:S(2)}) collective-permute-start(f32[3,2048]{1,0:T(4,128)S(1)} %collective-permute-done.1), channel_id=1, source_target_pairs={{0,4},{4,8},{8,12},{12,16},{16,20},{20,24},{24,28},{28,0},{1,5},{5... | collective-permute-start | bytes 73736 | tf_op jit(solution)/shard_map/ppermute | solution.py:75
  97.0 7.7 %collective-permute-start.3 = (f32[3,2048]{1,0:T(4,128)S(1)}, f32[3,2048]{1,0:T(4,128)S(1)}, u32[]{:S(2)}, u32[]{:S(2)}) collective-permute-start(f32[3,2048]{1,0:T(4,128)S(1)} %collective-permute-done.2), channel_id=1, source_target_pairs={{0,4},{4,8},{8,12},{12,16},{16,20},{20,24},{24,28},{28,0},{1,5},{5... | collective-permute-start | bytes 73736 | tf_op jit(solution)/shard_map/ppermute | solution.py:75
  104.7 6.7 %collective-permute-start.4 = (f32[3,2048]{1,0:T(4,128)S(1)}, f32[3,2048]{1,0:T(4,128)S(1)}, u32[]{:S(2)}, u32[]{:S(2)}) collective-permute-start(f32[3,2048]{1,0:T(4,128)S(1)} %collective-permute-done.3), channel_id=1, source_target_pairs={{0,4},{4,8},{8,12},{12,16},{16,20},{20,24},{24,28},{28,0},{1,5},{5... | collective-permute-start | bytes 73736 | tf_op jit(solution)/shard_map/ppermute | solution.py:75
  111.4 6.7 %collective-permute-start.5 = (f32[3,2048]{1,0:T(4,128)S(1)}, f32[3,2048]{1,0:T(4,128)S(1)}, u32[]{:S(2)}, u32[]{:S(2)}) collective-permute-start(f32[3,2048]{1,0:T(4,128)S(1)} %collective-permute-done.4), channel_id=1, source_target_pairs={{0,4},{4,8},{8,12},{12,16},{16,20},{20,24},{24,28},{28,0},{1,5},{5... | collective-permute-start | bytes 73736 | tf_op jit(solution)/shard_map/ppermute | solution.py:75
  118.1 6.6 %collective-permute-start.6 = (f32[3,2048]{1,0:T(4,128)S(1)}, f32[3,2048]{1,0:T(4,128)S(1)}, u32[]{:S(2)}, u32[]{:S(2)}) collective-permute-start(f32[3,2048]{1,0:T(4,128)S(1)} %collective-permute-done.5), channel_id=1, source_target_pairs={{0,4},{4,8},{8,12},{12,16},{16,20},{20,24},{24,28},{28,0},{1,5},{5... | collective-permute-start | bytes 73736 | tf_op jit(solution)/shard_map/ppermute | solution.py:75
  135.6 28.2 %all-to-all-start = ((f32[8,16,2048]{2,1,0:T(8,128)}), f32[8,16,2048]{2,1,0:T(8,128)S(1)}, u32[]{:S(2)}, u32[]{:S(2)}) async-start(f32[8,16,2048]{2,1,0:T(8,128)} %bitcast.2), calls=%async_computation.2 | async-start | bytes 2097152 | tf_op jit(solution)/shard_map/all_to_all | solution.py:79
Sparse Core Ops, SparseCore 0:
  10.1 42.8 all-gather.1
  75.7 72.0 reduce-scatter.2
  151.4 71.5 reduce-scatter.4
